TPU v7x, 32 devices: a whole 2x2x4 slice. The times are simulated.
32 devices in a mesh: tile: 16 (over z, x, core), rep: 2 (over y).
Axes of the slice: x: 2, y: 2, z: 4, core: 2. Of those that a mesh axis runs over, the one named last changes fastest.
Arguments:
- waves: bfloat16 [2, 8192, 128], P('rep', 'tile'), may hold values from -6 to 6
- dest_tile: int32 [2, 8192, 1], P('rep', 'tile'), may hold values from 0 to 15; in each aligned block of 512 rows (0 to 511, 512 to 1023, ..., all dimensions but the last counted through in order) at most 32 rows name the same one
- pixel_bin: int32 [2, 8192], P('rep', 'tile'), may hold values from 0 to 1023
- target: float32 [2, 128, 128], P('rep', 'tile'), may hold values from -6 to 6
- conv_one: bfloat16 [3, 3, 128, 128], replicated, may hold values from -0.1875 to 0.1875
- bias_one: float32 [128], replicated, may hold values from -0.5 to 0.5
- conv_two: bfloat16 [3, 3, 128], replicated, may hold values from -0.1875 to 0.1875
- bias_two: float32 [1], replicated, may hold values from -1 to 1
Outputs:
- prediction: float32 [2, 128, 128], P('rep', 'tile')
- update_one: float32 [3, 3, 128, 128], replicated
- update_bias: float32 [128], replicated
- update_two: float32 [3, 3, 128], replicated
Inputs may be any that keep to these rules, and one draw needn't show every extreme that they name: `dest_tile`: among the rows of one device, no strip is named more than 32 times, a bound that some block reaches.
All inputs are finite; a program needn't handle non-finite values.
Results may differ from a plain program's by a relative error of at most 0.0024.
The roundings to bfloat16 on the way count: a program that leaves them out, or rounds other values in their place, can miss the bound.
Values may be sent and summed in bfloat16 or wider, within the bound.
A program may use at most 64 MiB of HBM per device.

v0:
```python
import math
import jax
import jax.numpy as jnp
from jax import lax
from jax.sharding import PartitionSpec as P

CAP = 32


def extended(block, sides, width):
    for axis, dim in sides:
        count = lax.axis_size(axis)
        forward = [(i, i + 1) for i in range(count - 1)]
        backward = [(target, source) for source, target in forward]
        low = lax.ppermute(
            lax.slice_in_dim(block, block.shape[dim] - width, None, axis=dim), axis, forward
        )
        high = lax.ppermute(lax.slice_in_dim(block, 0, width, axis=dim), axis, backward)
        block = jnp.concatenate([low, block, high], axis=dim)
    return block


def normalized(grad):
    return grad / jnp.sqrt(jnp.mean(grad * grad) + 1e-06)


def first_conv(padded, conv_one, bias_one, tall, width):
    steps = padded.shape[2]
    channels = conv_one.shape[3]
    pre = jnp.zeros((tall * width, channels), jnp.float32) + bias_one[None, :]
    for i in range(3):
        for j in range(3):
            patch = padded[2 * i : 2 * i + tall, 2 * j : 2 * j + width, :].reshape(
                tall * width, steps
            )
            pre = pre + jnp.dot(patch, conv_one[i, j], preferred_element_type=jnp.float32)
    return pre.reshape(tall, width, channels)


def second_conv(hidden_pad, conv_two, bias_two, tall, width):
    pred = jnp.zeros((tall, width), jnp.float32) + bias_two[0]
    for i in range(3):
        for j in range(3):
            pred = pred + jnp.einsum(
                "hwc,c->hw",
                hidden_pad[i : i + tall, j : j + width, :],
                conv_two[i, j],
                preferred_element_type=jnp.float32,
            )
    return pred


def on_device(waves, dest_tile, pixel_bin, target, conv_one, bias_one, conv_two, bias_two):
    tiles = lax.axis_size("tile")
    replicas = lax.axis_size("rep")
    steps = waves.shape[2]
    height = target.shape[1]
    width = target.shape[2]
    pixels = height * width
    channels = conv_one.shape[3]
    bucket = CAP
    tile_ids = dest_tile[0, :, 0]
    hits = (tile_ids[:, None] == jnp.arange(tiles, dtype=jnp.int32)[None, :]).astype(jnp.int32)
    rank = jnp.sum(jnp.cumsum(hits, axis=0) * hits, axis=1) - 1
    slots = tile_ids * bucket + rank
    send_wave = jnp.zeros((tiles * bucket, steps), jnp.bfloat16).at[slots].set(waves[0])
    send_bin = jnp.full((tiles * bucket,), -1, jnp.int32).at[slots].set(pixel_bin[0])
    recv_wave, recv_bin = (
        lax.all_to_all(
            send_wave.reshape(tiles, bucket, steps), "tile", split_axis=0, concat_axis=0, tiled=True
        ),
        lax.all_to_all(
            send_bin.reshape(tiles, bucket), "tile", split_axis=0, concat_axis=0, tiled=True
        ),
    )
    recv_wave = recv_wave.reshape(tiles * bucket, steps)
    recv_bin = recv_bin.reshape(tiles * bucket)
    block = math.gcd(pixels, 128)

    def raster(start):
        wanted = start + jnp.arange(block, dtype=jnp.int32)
        onehot = (wanted[:, None] == recv_bin[None, :]).astype(jnp.bfloat16)
        return jnp.dot(onehot, recv_wave, preferred_element_type=jnp.float32).astype(jnp.bfloat16)

    starts = jnp.arange(0, pixels, block, dtype=jnp.int32)
    grid = lax.map(raster, starts)
    padded = extended(grid, (("tile", 0),), 2)
    padded = jnp.pad(padded, ((0, 0), (2, 2), (0, 0)))
    pre = first_conv(padded, conv_one, bias_one, height, width)
    hidden = jax.nn.silu(pre).astype(jnp.bfloat16)
    hidden_pad = extended(hidden, (("tile", 0),), 1)
    hidden_pad = jnp.pad(hidden_pad, ((0, 0), (1, 1), (0, 0)))
    pred = second_conv(hidden_pad, conv_two, bias_two, height, width)
    error = ((pred - target[0]) / replicas).astype(jnp.bfloat16)
    error_pad = extended(error, (("tile", 0),), 1)
    error_pad = jnp.pad(error_pad, ((0, 0), (1, 1)))
    grad_two = []
    back = jnp.zeros((height, width, channels), jnp.float32)
    for i in range(3):
        for j in range(3):
            grad_two.append(
                jnp.einsum(
                    "hwc,hw->c",
                    hidden_pad[i : i + height, j : j + width, :],
                    error,
                    preferred_element_type=jnp.float32,
                )
            )
            shifted = error_pad[2 - i : 2 - i + height, 2 - j : 2 - j + width].astype(jnp.float32)
            back = back + shifted[:, :, None] * conv_two[i, j].astype(jnp.float32)[None, None, :]
    grad_two = jnp.stack(grad_two).reshape(3, 3, channels)
    sig = jax.nn.sigmoid(pre)
    slope = (back * sig * (1.0 + pre * (1.0 - sig))).astype(jnp.bfloat16)
    slope_flat = slope.reshape(pixels, channels)
    grad_one = []
    for i in range(3):
        for j in range(3):
            patch = padded[2 * i : 2 * i + height, 2 * j : 2 * j + width, :].reshape(pixels, steps)
            grad_one.append(
                lax.dot_general(
                    patch, slope_flat, (((0,), (0,)), ((), ())), preferred_element_type=jnp.float32
                )
            )
    grad_one = jnp.stack(grad_one).reshape(3, 3, steps, channels)
    grad_bias = jnp.sum(slope_flat.astype(jnp.float32), axis=0)
    share = lax.psum_scatter(
        grad_one.reshape(9 * steps, channels), "tile", scatter_dimension=0, tiled=True
    )
    share = lax.psum(share, "rep")
    grad_one = lax.all_gather(share, "tile", axis=0, tiled=True).reshape(3, 3, steps, channels)
    grad_bias, grad_two = lax.psum((grad_bias, grad_two), ("tile", "rep"))
    return (pred[None], normalized(grad_one), normalized(grad_bias), normalized(grad_two))


def solution(mesh):
    placed = (
        P("rep", "tile", None),
        P("rep", "tile", None),
        P("rep", "tile"),
        P("rep", "tile", None),
        P(),
        P(),
        P(),
        P(),
    )
    return jax.shard_map(
        on_device,
        mesh=mesh,
        in_specs=placed,
        out_specs=(P("rep", "tile", None), P(), P(), P()),
        check_vma=False,
    )
```

profile of v0, /device:TPU:0, one launch (start us, length us, event | category | flops | bytes accessed | tf_op | source)
XLA Modules:
  0.0 186.0 jit_solution(650408584183058171)
XLA Ops:
  7.9 1.1 reduce-window.6
  10.8 2.6 %scatter_custom_fusion = s32[512]{0:T(512)S(1)} fusion(s32[512]{0:T(512)S(1)} %bitcast.330, s32[512]{0:T(512)} %bitcast.332, s32[]{:T(128)} %constant.22.clone.1), kind=kCustom, calls=%fused_computation.156 | custom fusion | bytes 2560 | tf_op jit(solution)/shard_map/scatter | solution.py:67
  14.1 7.4 %all-to-all-start = ((s32[16,1,32]{2,1,0:T(1,128)}), s32[16,1,32]{2,1,0:T(1,128)S(1)}, u32[]{:S(2)}, u32[]{:S(2)}) async-start(s32[16,1,32]{2,1,0:T(1,128)} %all_to_all.11), calls=%async_computation | async-start | bytes 16384 | tf_op jit(solution)/shard_map/all_to_all | solution.py:72
  21.4 2.4 %scatter_custom_fusion.1 = bf16[512,128]{1,0:T(8,128)(2,1)} fusion(s32[512]{0:T(512)S(1)} %bitcast.331, bf16[1,512,128]{2,1,0:T(8,128)(2,1)S(1)} %copy-done, bf16[]{:T(256)} %constant.14.clone.1), kind=kCustom, calls=%fused_computation.100 | custom fusion | bytes 262146 | tf_op jit(solution)/shard_map/scatter | solution.py:66
  23.8 4.0 %all-to-all-done = s32[16,1,32]{2,1,0:T(1,128)S(1)} async-done(((s32[16,1,32]{2,1,0:T(1,128)}), s32[16,1,32]{2,1,0:T(1,128)S(1)}, u32[]{:S(2)}, u32[]{:S(2)}) %all-to-all-start) | async-done | bytes 2080 | tf_op jit(solution)/shard_map/all_to_all | solution.py:72
  27.8 3.5 %all-to-all-start.1 = ((bf16[16,32,128]{2,1,0:T(8,128)(2,1)}), bf16[16,32,128]{2,1,0:T(8,128)(2,1)S(1)}, u32[]{:S(2)}, u32[]{:S(2)}) async-start(bf16[16,32,128]{2,1,0:T(8,128)(2,1)} %bitcast.12), calls=%async_computation.1 | async-start | bytes 262144 | tf_op jit(solution)/shard_map/all_to_all | solution.py:69
  31.5 7.8 %all-to-all-done.1 = bf16[16,32,128]{2,1,0:T(8,128)(2,1)S(1)} async-done(((bf16[16,32,128]{2,1,0:T(8,128)(2,1)}), bf16[16,32,128]{2,1,0:T(8,128)(2,1)S(1)}, u32[]{:S(2)}, u32[]{:S(2)}) %all-to-all-start.1) | async-done | bytes 131104 | tf_op jit(solution)/shard_map/all_to_all | solution.py:69
  39.3 12.0 %while.11 = (s32[]{:T(128)}, bf16[8,128,128]{2,1,0:T(8,128)(2,1)S(1)}, s32[8]{0:T(128)S(1)}, s32[16,32]{1,0:T(8,128)}, bf16[512,128]{1,0:T(8,128)(2,1)S(1)}, /*index=5*/s32[512]{0:T(512)S(1)}, s32[]{:T(128)}) while((s32[]{:T(128)}, bf16[8,128,128]{2,1,0:T(8,128)(2,1)S(1)}, s32[8]{0:T(128)S(1)}, s32[16,32]{1,0:T(8,128)}, ...), condition=%wide.wide.region_6.7_spmd, body=%wide.wide.region_5.6_spmd.sunk | while | flops 16859264 | bytes 167009 | solution.py:86
  51.5 1.3 collective-permute-start
  52.8 1.3 collective-permute-start.1
  57.6 0.9 pad_maximum_fusion.2
  61.2 1.0 convolution_add_fusion.8
  65.0 4.4 %collective-permute-start.2 = (bf16[1,128,128]{2,1,0:T(8,128)(2,1)S(1)}, bf16[1,128,128]{2,1,0:T(8,128)(2,1)S(1)}, u32[]{:S(2)}, u32[]{:S(2)}) collective-permute-start(bf16[1,128,128]{2,1,0:T(8,128)(2,1)S(1)} %get-tuple-element.53), channel_id=1, source_target_pairs={{0,2},{2,4},{4,6},{6,8},{8,10},{10,12},{12,14},{14,16},{16,18},{18... | collective-permute-start | bytes 98312 | tf_op jit(solution)/shard_map/ppermute | solution.py:15
  69.4 1.3 collective-permute-start.3
  70.8 1.6 collective-permute-done.3
  76.0 4.8 %collective-permute-start.4 = (bf16[1,128]{1,0:T(2,128)(2,1)S(1)}, bf16[1,128]{1,0:T(2,128)(2,1)S(1)}, u32[]{:S(2)}, u32[]{:S(2)}) collective-permute-start(bf16[1,128]{1,0:T(2,128)(2,1)S(1)} %get-tuple-element.87), channel_id=1, source_target_pairs={{0,2},{2,4},{4,6},{6,8},{8,10},{10,12},{12,14},{14,16},{16,18},{18... | collective-permute-start | bytes 776 | tf_op jit(solution)/shard_map/ppermute | solution.py:15
  80.8 1.3 collective-permute-start.5
  82.4 1.4 collective-permute-done.5
  84.0 1.6 multiply_convert_fusion.1
  88.8 1.6 convert_reduce_fusion
  90.5 42.7 %all-reduce.4 = (f32[128]{0:T(128)S(1)}, f32[3,3,128]{2,1,0:T(4,128)S(1)}) all-reduce(f32[128]{0:T(128)S(1)} %convert_reduce_fusion, f32[3,3,128]{2,1,0:T(4,128)S(1)} %reshape.152), channel_id=1, replica_groups=mesh['tile'=16,'rep'=2] {'tile','rep'}, use_global_device_ids=true, to_apply=%region_11.12 | all-reduce | flops 1280 | bytes 10240 | tf_op jit(solution)/shard_map/psum | solution.py:131
  136.9 9.8 %reduce-scatter.4.cloned.1.call-done = f32[72,128]{1,0:T(8,128)} async-done(((f32[1152,128]{1,0:T(8,128)}), f32[72,128]{1,0:T(8,128)}) %reduce-scatter.4.cloned.1.call-update) | async-done | bytes 36880
  146.7 9.1 %psum.21 = f32[72,128]{1,0:T(8,128)S(1)} all-reduce(f32[72,128]{1,0:T(8,128)} %reduce-scatter.4.cloned.1.call-done), channel_id=1, replica_groups=mesh['tile'=16,'rep'=2] {'rep'}, use_global_device_ids=true, to_apply=%region_8.9 | all-reduce | flops 9216 | bytes 73728 | tf_op jit(solution)/shard_map/psum | solution.py:129
  155.8 21.1 %all_gather.3 = f32[1152,128]{1,0:T(8,128)S(1)} all-gather(f32[72,128]{1,0:T(8,128)S(1)} %psum.21), channel_id=1, replica_groups=mesh['tile'=16,'rep'=2] {'tile'}, dimensions={0}, use_global_device_ids=true | all-gather | bytes 626688 | tf_op jit(solution)/shard_map/all_gather | solution.py:130
  (141 shorter events, 34.6 us)
Async XLA Ops:
  7.2 14.3 %copy-start = (bf16[1,512,128]{2,1,0:T(8,128)(2,1)S(1)}, bf16[1,512,128]{2,1,0:T(8,128)(2,1)}, u32[]{:S(2)}) copy-start(bf16[1,512,128]{2,1,0:T(8,128)(2,1)} %param.10) | copy-start | bytes 393220
  14.1 13.8 %all-to-all-start = ((s32[16,1,32]{2,1,0:T(1,128)}), s32[16,1,32]{2,1,0:T(1,128)S(1)}, u32[]{:S(2)}, u32[]{:S(2)}) async-start(s32[16,1,32]{2,1,0:T(1,128)} %all_to_all.11), calls=%async_computation | async-start | bytes 16384 | tf_op jit(solution)/shard_map/all_to_all | solution.py:72
  27.8 11.4 %copy-start.9 = (s32[16,1,32]{2,1,0:T(1,128)}, s32[16,1,32]{2,1,0:T(1,128)S(1)}, u32[]{:S(2)}) copy-start(s32[16,1,32]{2,1,0:T(1,128)S(1)} %all-to-all-done) | copy-start | bytes 6148
  27.8 11.4 %all-to-all-start.1 = ((bf16[16,32,128]{2,1,0:T(8,128)(2,1)}), bf16[16,32,128]{2,1,0:T(8,128)(2,1)S(1)}, u32[]{:S(2)}, u32[]{:S(2)}) async-start(bf16[16,32,128]{2,1,0:T(8,128)(2,1)} %bitcast.12), calls=%async_computation.1 | async-start | bytes 262144 | tf_op jit(solution)/shard_map/all_to_all | solution.py:69
  31.4 115.3 %reduce-scatter.4.cloned.1.call-start = ((), (), s32[]{:S(2)}) async-start(), calls=%async_computation.3 | async-start | bytes 626688
  39.3 14.9 %copy-start.10 = (bf16[3,3,128]{2,1,0:T(4,128)(2,1)S(1)}, bf16[3,3,128]{2,1,0:T(4,128)(2,1)}, u32[]{:S(2)}) copy-start(bf16[3,3,128]{2,1,0:T(4,128)(2,1)} %param.16) | copy-start | bytes 6916
  51.5 3.9 %collective-permute-start = (bf16[2,128,128]{1,2,0:T(8,128)(2,1)S(1)}, bf16[2,128,128]{1,2,0:T(8,128)(2,1)S(1)}, u32[]{:S(2)}, u32[]{:S(2)}) collective-permute-start(bf16[2,128,128]{1,2,0:T(8,128)(2,1)S(1)} %get-tuple-element.57), channel_id=1, source_target_pairs={{0,2},{2,4},{4,6},{6,8},{8,10},{10,12},{12,14},{14,16},{16,18},{18... | collective-permute-start | bytes 196616 | tf_op jit(solution)/shard_map/ppermute | solution.py:15
  52.8 3.1 %collective-permute-start.1 = (bf16[2,128,128]{1,2,0:T(8,128)(2,1)S(1)}, bf16[2,128,128]{1,2,0:T(8,128)(2,1)S(1)}, u32[]{:S(2)}, u32[]{:S(2)}) collective-permute-start(bf16[2,128,128]{1,2,0:T(8,128)(2,1)S(1)} %get-tuple-element.58), channel_id=1, source_target_pairs={{2,0},{4,2},{6,4},{8,6},{10,8},{12,10},{14,12},{16,14},{18,16},{20... | collective-permute-start | bytes 196616 | tf_op jit(solution)/shard_map/ppermute | solution.py:18
  61.0 1.3 copy-start.2
  61.2 1.1 copy-start.8
  62.3 1.0 copy-start.1
  65.0 5.9 %collective-permute-start.2 = (bf16[1,128,128]{2,1,0:T(8,128)(2,1)S(1)}, bf16[1,128,128]{2,1,0:T(8,128)(2,1)S(1)}, u32[]{:S(2)}, u32[]{:S(2)}) collective-permute-start(bf16[1,128,128]{2,1,0:T(8,128)(2,1)S(1)} %get-tuple-element.53), channel_id=1, source_target_pairs={{0,2},{2,4},{4,6},{6,8},{8,10},{10,12},{12,14},{14,16},{16,18},{18... | collective-permute-start | bytes 98312 | tf_op jit(solution)/shard_map/ppermute | solution.py:15
  69.4 3.1 %collective-permute-start.3 = (bf16[1,128,128]{2,1,0:T(8,128)(2,1)S(1)}, bf16[1,128,128]{2,1,0:T(8,128)(2,1)S(1)}, u32[]{:S(2)}, u32[]{:S(2)}) collective-permute-start(bf16[1,128,128]{2,1,0:T(8,128)(2,1)S(1)} %get-tuple-element.54), channel_id=1, source_target_pairs={{2,0},{4,2},{6,4},{8,6},{10,8},{12,10},{14,12},{16,14},{18,16},{20... | collective-permute-start | bytes 98312 | tf_op jit(solution)/shard_map/ppermute | solution.py:18
  75.8 8.2 %copy-start.11 = (f32[128]{0:T(128)S(1)}, f32[128]{0:T(128)}, u32[]{:S(2)}) copy-start(f32[128]{0:T(128)} %get-tuple-element.74) | copy-start | bytes 1540
  75.8 8.2 %copy-start.12 = (f32[128]{0:T(128)S(1)}, f32[128]{0:T(128)}, u32[]{:S(2)}) copy-start(f32[128]{0:T(128)} %get-tuple-element.75) | copy-start | bytes 1540
  75.8 8.2 %copy-start.13 = (f32[128]{0:T(128)S(1)}, f32[128]{0:T(128)}, u32[]{:S(2)}) copy-start(f32[128]{0:T(128)} %get-tuple-element.76) | copy-start | bytes 1540
  75.8 8.2 %copy-start.14 = (f32[128]{0:T(128)S(1)}, f32[128]{0:T(128)}, u32[]{:S(2)}) copy-start(f32[128]{0:T(128)} %get-tuple-element.77) | copy-start | bytes 1540
  75.8 8.2 %copy-start.15 = (f32[128]{0:T(128)S(1)}, f32[128]{0:T(128)}, u32[]{:S(2)}) copy-start(f32[128]{0:T(128)} %get-tuple-element.78) | copy-start | bytes 1540
  75.8 8.2 %copy-start.16 = (f32[128]{0:T(128)S(1)}, f32[128]{0:T(128)}, u32[]{:S(2)}) copy-start(f32[128]{0:T(128)} %get-tuple-element.79) | copy-start | bytes 1540
  76.0 6.5 %collective-permute-start.4 = (bf16[1,128]{1,0:T(2,128)(2,1)S(1)}, bf16[1,128]{1,0:T(2,128)(2,1)S(1)}, u32[]{:S(2)}, u32[]{:S(2)}) collective-permute-start(bf16[1,128]{1,0:T(2,128)(2,1)S(1)} %get-tuple-element.87), channel_id=1, source_target_pairs={{0,2},{2,4},{4,6},{6,8},{8,10},{10,12},{12,14},{14,16},{16,18},{18... | collective-permute-start | bytes 776 | tf_op jit(solution)/shard_map/ppermute | solution.py:15
  80.8 3.0 %collective-permute-start.5 = (bf16[1,128]{1,0:T(2,128)(2,1)S(1)}, bf16[1,128]{1,0:T(2,128)(2,1)S(1)}, u32[]{:S(2)}, u32[]{:S(2)}) collective-permute-start(bf16[1,128]{1,0:T(2,128)(2,1)S(1)} %get-tuple-element.88), channel_id=1, source_target_pairs={{2,0},{4,2},{6,4},{8,6},{10,8},{12,10},{14,12},{16,14},{18,16},{20... | collective-permute-start | bytes 776 | tf_op jit(solution)/shard_map/ppermute | solution.py:18
  82.4 3.5 %copy-start.7 = (bf16[2,128,128]{1,2,0:T(8,128)(2,1)S(1)}, bf16[2,128,128]{1,2,0:T(8,128)(2,1)}, u32[]{:S(2)}) copy-start(bf16[2,128,128]{1,2,0:T(8,128)(2,1)} %copy-done.6) | copy-start | bytes 196612
  86.6 0.8 copy-start.5
  88.0 0.8 copy-start.3
  (3 other events, 2.0 us)
Sparse Core Ops, SparseCore 0:
  88.9 57.6 reduce-scatter.3
where the time goes:
time: 187 us; the launch traced here: 186 us
  blocking collectives  72.9 us (39%)
  starting transfers between devices  25.2 us (13%)
  waiting for transfers between devices  25.2 us (13%)
  other arithmetic  18.6 us (10%)
  between operations  17.3 us (9%)
  local copies, waits for them, and re-layouts  16.5 us (9%)
  matrix products  10.1 us (5%)
    psum x1, blocking collectives, on_device(): grad_bias, grad_two = lax.psum((grad_bias, grad_two), ('tile', 'rep'))  42.7 us
    all_gather x1, blocking collectives, on_device(): lax.all_gather(share, 'tile', axis=0, tiled=True)  21.1 us
    ppermute x3, starting transfers between devices, extended(): lax.ppermute(lax.slice_in_dim(block, block.shape[dim] - width, None, axis...  10.5 us
    unnamed x2, waiting for transfers between devices  9.84 us
    psum x1, blocking collectives, on_device(): share = lax.psum(share, 'rep')  9.1 us
    all_to_all x1, waiting for transfers between devices, on_device(): lax.all_to_all(send_wave.reshape(tiles, bucket, steps), 'tile', split_axi...  7.75 us
    all_to_all x1, starting transfers between devices, on_device(): lax.all_to_all(send_bin.reshape(tiles, bucket), 'tile', split_axis=0, con...  7.36 us
    add x8, other arithmetic, raster(): wanted = start + jnp.arange(block, dtype=jnp.int32)  5.17 us
  transfers between devices with their start and end apart: 9, of which 6 were waited for; matrix products, arithmetic and copies ran while one was open for 4% of the time, Pallas kernels for 0%

commit v1 on v0

--- a/solution.py
+++ b/solution.py
@@ -126,7 +126,7 @@
     share = lax.psum_scatter(
         grad_one.reshape(9 * steps, channels), "tile", scatter_dimension=0, tiled=True
     )
-    share = lax.psum(share, "rep")
+    share = jnp.sum(lax.all_gather(share, "rep"), axis=0)
     grad_one = lax.all_gather(share, "tile", axis=0, tiled=True).reshape(3, 3, steps, channels)
     grad_bias, grad_two = lax.psum((grad_bias, grad_two), ("tile", "rep"))
     return (pred[None], normalized(grad_one), normalized(grad_bias), normalized(grad_two))

time: 187 us -> 183 us (0.979)
  blocking collectives: 72.9 us -> 68.6 us
    psum x1 -> x0, blocking collectives: 9.1 us -> none  [on_device(): share = lax.psum(share, 'rep')]
    all_gather x0 -> x1, blocking collectives: none -> 4.83 us  [on_device(): share = jnp.sum(lax.all_gather(share, 'rep'), axis=0)]
where the time goes in v1:
time: 183 us; the launch traced here: 182 us
  blocking collectives  68.6 us (37%)
  starting transfers between devices  25.2 us (14%)
  waiting for transfers between devices  25.2 us (14%)
  other arithmetic  18.6 us (10%)
  between operations  17.3 us (9%)
  local copies, waits for them, and re-layouts  16.5 us (9%)
  matrix products  10.1 us (6%)
    psum x1, blocking collectives, on_device(): grad_bias, grad_two = lax.psum((grad_bias, grad_two), ('tile', 'rep'))  42.7 us
    all_gather x1, blocking collectives, on_device(): lax.all_gather(share, 'tile', axis=0, tiled=True)  21.1 us
    ppermute x3, starting transfers between devices, extended(): lax.ppermute(lax.slice_in_dim(block, block.shape[dim] - width, None, axis...  10.5 us
    unnamed x2, waiting for transfers between devices  9.84 us
    all_to_all x1, waiting for transfers between devices, on_device(): lax.all_to_all(send_wave.reshape(tiles, bucket, steps), 'tile', split_axi...  7.75 us
    all_to_all x1, starting transfers between devices, on_device(): lax.all_to_all(send_bin.reshape(tiles, bucket), 'tile', split_axis=0, con...  7.36 us
    add x8, other arithmetic, raster(): wanted = start + jnp.arange(block, dtype=jnp.int32)  5.17 us
    all_gather x1, blocking collectives, on_device(): share = jnp.sum(lax.all_gather(share, 'rep'), axis=0)  4.83 us
  transfers between devices with their start and end apart: 9, of which 6 were waited for; matrix products, arithmetic and copies ran while one was open for 4% of the time, Pallas kernels for 0%

profile of v1, /device:TPU:0, one launch (start us, length us, event | category | flops | bytes accessed | tf_op | source)
XLA Modules:
  0.0 181.8 jit_solution(10842800331650394176)
XLA Ops:
  7.9 1.1 reduce-window.6
  10.8 2.6 %scatter_custom_fusion = s32[512]{0:T(512)S(1)} fusion(s32[512]{0:T(512)S(1)} %bitcast.332, s32[512]{0:T(512)} %bitcast.334, s32[]{:T(128)} %constant.22.clone.1), kind=kCustom, calls=%fused_computation.156 | custom fusion | bytes 2560 | tf_op jit(solution)/shard_map/scatter | solution.py:67
  14.1 7.4 %all-to-all-start = ((s32[16,1,32]{2,1,0:T(1,128)}), s32[16,1,32]{2,1,0:T(1,128)S(1)}, u32[]{:S(2)}, u32[]{:S(2)}) async-start(s32[16,1,32]{2,1,0:T(1,128)} %all_to_all.11), calls=%async_computation | async-start | bytes 16384 | tf_op jit(solution)/shard_map/all_to_all | solution.py:72
  21.4 2.4 %scatter_custom_fusion.1 = bf16[512,128]{1,0:T(8,128)(2,1)} fusion(s32[512]{0:T(512)S(1)} %bitcast.333, bf16[1,512,128]{2,1,0:T(8,128)(2,1)S(1)} %copy-done, bf16[]{:T(256)} %constant.14.clone.1), kind=kCustom, calls=%fused_computation.100 | custom fusion | bytes 262146 | tf_op jit(solution)/shard_map/scatter | solution.py:66
  23.8 4.0 %all-to-all-done = s32[16,1,32]{2,1,0:T(1,128)S(1)} async-done(((s32[16,1,32]{2,1,0:T(1,128)}), s32[16,1,32]{2,1,0:T(1,128)S(1)}, u32[]{:S(2)}, u32[]{:S(2)}) %all-to-all-start) | async-done | bytes 2080 | tf_op jit(solution)/shard_map/all_to_all | solution.py:72
  27.8 3.5 %all-to-all-start.1 = ((bf16[16,32,128]{2,1,0:T(8,128)(2,1)}), bf16[16,32,128]{2,1,0:T(8,128)(2,1)S(1)}, u32[]{:S(2)}, u32[]{:S(2)}) async-start(bf16[16,32,128]{2,1,0:T(8,128)(2,1)} %bitcast.12), calls=%async_computation.1 | async-start | bytes 262144 | tf_op jit(solution)/shard_map/all_to_all | solution.py:69
  31.5 7.8 %all-to-all-done.1 = bf16[16,32,128]{2,1,0:T(8,128)(2,1)S(1)} async-done(((bf16[16,32,128]{2,1,0:T(8,128)(2,1)}), bf16[16,32,128]{2,1,0:T(8,128)(2,1)S(1)}, u32[]{:S(2)}, u32[]{:S(2)}) %all-to-all-start.1) | async-done | bytes 131104 | tf_op jit(solution)/shard_map/all_to_all | solution.py:69
  39.3 12.0 %while.11 = (s32[]{:T(128)}, bf16[8,128,128]{2,1,0:T(8,128)(2,1)S(1)}, s32[8]{0:T(128)S(1)}, s32[16,32]{1,0:T(8,128)}, bf16[512,128]{1,0:T(8,128)(2,1)S(1)}, /*index=5*/s32[512]{0:T(512)S(1)}, s32[]{:T(128)}) while((s32[]{:T(128)}, bf16[8,128,128]{2,1,0:T(8,128)(2,1)S(1)}, s32[8]{0:T(128)S(1)}, s32[16,32]{1,0:T(8,128)}, ...), condition=%wide.wide.region_6.7_spmd, body=%wide.wide.region_5.6_spmd.sunk | while | flops 16859264 | bytes 167009 | solution.py:86
  51.5 1.3 collective-permute-start
  52.8 1.3 collective-permute-start.1
  57.6 0.9 pad_maximum_fusion.2
  61.2 1.0 convolution_add_fusion.8
  65.0 4.4 %collective-permute-start.2 = (bf16[1,128,128]{2,1,0:T(8,128)(2,1)S(1)}, bf16[1,128,128]{2,1,0:T(8,128)(2,1)S(1)}, u32[]{:S(2)}, u32[]{:S(2)}) collective-permute-start(bf16[1,128,128]{2,1,0:T(8,128)(2,1)S(1)} %get-tuple-element.53), channel_id=1, source_target_pairs={{0,2},{2,4},{4,6},{6,8},{8,10},{10,12},{12,14},{14,16},{16,18},{18... | collective-permute-start | bytes 98312 | tf_op jit(solution)/shard_map/ppermute | solution.py:15
  69.4 1.3 collective-permute-start.3
  70.8 1.6 collective-permute-done.3
  76.0 4.8 %collective-permute-start.4 = (bf16[1,128]{1,0:T(2,128)(2,1)S(1)}, bf16[1,128]{1,0:T(2,128)(2,1)S(1)}, u32[]{:S(2)}, u32[]{:S(2)}) collective-permute-start(bf16[1,128]{1,0:T(2,128)(2,1)S(1)} %get-tuple-element.87), channel_id=1, source_target_pairs={{0,2},{2,4},{4,6},{6,8},{8,10},{10,12},{12,14},{14,16},{16,18},{18... | collective-permute-start | bytes 776 | tf_op jit(solution)/shard_map/ppermute | solution.py:15
  80.8 1.3 collective-permute-start.5
  82.4 1.4 collective-permute-done.5
  84.0 1.6 multiply_convert_fusion.1
  88.8 1.6 convert_reduce_fusion
  90.5 42.7 %all-reduce.4 = (f32[128]{0:T(128)S(1)}, f32[3,3,128]{2,1,0:T(4,128)S(1)}) all-reduce(f32[128]{0:T(128)S(1)} %convert_reduce_fusion, f32[3,3,128]{2,1,0:T(4,128)S(1)} %reshape.152), channel_id=1, replica_groups=mesh['tile'=16,'rep'=2] {'tile','rep'}, use_global_device_ids=true, to_apply=%region_11.12 | all-reduce | flops 1280 | bytes 10240 | tf_op jit(solution)/shard_map/psum | solution.py:131
  136.9 9.8 %reduce-scatter.4.cloned.1.call-done = f32[72,128]{1,0:T(8,128)} async-done(((f32[1152,128]{1,0:T(8,128)}), f32[72,128]{1,0:T(8,128)}) %reduce-scatter.4.cloned.1.call-update) | async-done | bytes 36880
  146.7 4.8 %all-gather = f32[144,128]{1,0:T(8,128)S(1)} all-gather(f32[72,128]{1,0:T(8,128)} %reduce-scatter.4.cloned.1.call-done), channel_id=2, replica_groups=mesh['tile'=16,'rep'=2] {'rep'}, dimensions={0}, use_global_device_ids=true | all-gather | bytes 110592 | tf_op jit(solution)/shard_map/all_gather | solution.py:129
  151.5 21.1 %all_gather.11 = f32[1152,128]{1,0:T(8,128)S(1)} all-gather(f32[72,128]{1,0:T(8,128)S(1)} %reduce_sum.55), channel_id=1, replica_groups=mesh['tile'=16,'rep'=2] {'tile'}, dimensions={0}, use_global_device_ids=true | all-gather | bytes 626688 | tf_op jit(solution)/shard_map/all_gather | solution.py:130
  (142 shorter events, 34.6 us)
Async XLA Ops:
  7.2 14.3 %copy-start = (bf16[1,512,128]{2,1,0:T(8,128)(2,1)S(1)}, bf16[1,512,128]{2,1,0:T(8,128)(2,1)}, u32[]{:S(2)}) copy-start(bf16[1,512,128]{2,1,0:T(8,128)(2,1)} %param.10) | copy-start | bytes 393220
  14.1 13.8 %all-to-all-start = ((s32[16,1,32]{2,1,0:T(1,128)}), s32[16,1,32]{2,1,0:T(1,128)S(1)}, u32[]{:S(2)}, u32[]{:S(2)}) async-start(s32[16,1,32]{2,1,0:T(1,128)} %all_to_all.11), calls=%async_computation | async-start | bytes 16384 | tf_op jit(solution)/shard_map/all_to_all | solution.py:72
  27.8 11.4 %copy-start.9 = (s32[16,1,32]{2,1,0:T(1,128)}, s32[16,1,32]{2,1,0:T(1,128)S(1)}, u32[]{:S(2)}) copy-start(s32[16,1,32]{2,1,0:T(1,128)S(1)} %all-to-all-done) | copy-start | bytes 6148
  27.8 11.4 %all-to-all-start.1 = ((bf16[16,32,128]{2,1,0:T(8,128)(2,1)}), bf16[16,32,128]{2,1,0:T(8,128)(2,1)S(1)}, u32[]{:S(2)}, u32[]{:S(2)}) async-start(bf16[16,32,128]{2,1,0:T(8,128)(2,1)} %bitcast.12), calls=%async_computation.1 | async-start | bytes 262144 | tf_op jit(solution)/shard_map/all_to_all | solution.py:69
  31.4 115.3 %reduce-scatter.4.cloned.1.call-start = ((), (), s32[]{:S(2)}) async-start(), calls=%async_computation.3 | async-start | bytes 626688
  39.3 14.9 %copy-start.10 = (bf16[3,3,128]{2,1,0:T(4,128)(2,1)S(1)}, bf16[3,3,128]{2,1,0:T(4,128)(2,1)}, u32[]{:S(2)}) copy-start(bf16[3,3,128]{2,1,0:T(4,128)(2,1)} %param.16) | copy-start | bytes 6916
  51.5 3.9 %collective-permute-start = (bf16[2,128,128]{1,2,0:T(8,128)(2,1)S(1)}, bf16[2,128,128]{1,2,0:T(8,128)(2,1)S(1)}, u32[]{:S(2)}, u32[]{:S(2)}) collective-permute-start(bf16[2,128,128]{1,2,0:T(8,128)(2,1)S(1)} %get-tuple-element.57), channel_id=1, source_target_pairs={{0,2},{2,4},{4,6},{6,8},{8,10},{10,12},{12,14},{14,16},{16,18},{18... | collective-permute-start | bytes 196616 | tf_op jit(solution)/shard_map/ppermute | solution.py:15
  52.8 3.1 %collective-permute-start.1 = (bf16[2,128,128]{1,2,0:T(8,128)(2,1)S(1)}, bf16[2,128,128]{1,2,0:T(8,128)(2,1)S(1)}, u32[]{:S(2)}, u32[]{:S(2)}) collective-permute-start(bf16[2,128,128]{1,2,0:T(8,128)(2,1)S(1)} %get-tuple-element.58), channel_id=1, source_target_pairs={{2,0},{4,2},{6,4},{8,6},{10,8},{12,10},{14,12},{16,14},{18,16},{20... | collective-permute-start | bytes 196616 | tf_op jit(solution)/shard_map/ppermute | solution.py:18
  61.0 1.3 copy-start.2
  61.2 1.1 copy-start.8
  62.3 1.0 copy-start.1
  65.0 5.9 %collective-permute-start.2 = (bf16[1,128,128]{2,1,0:T(8,128)(2,1)S(1)}, bf16[1,128,128]{2,1,0:T(8,128)(2,1)S(1)}, u32[]{:S(2)}, u32[]{:S(2)}) collective-permute-start(bf16[1,128,128]{2,1,0:T(8,128)(2,1)S(1)} %get-tuple-element.53), channel_id=1, source_target_pairs={{0,2},{2,4},{4,6},{6,8},{8,10},{10,12},{12,14},{14,16},{16,18},{18... | collective-permute-start | bytes 98312 | tf_op jit(solution)/shard_map/ppermute | solution.py:15
  69.4 3.1 %collective-permute-start.3 = (bf16[1,128,128]{2,1,0:T(8,128)(2,1)S(1)}, bf16[1,128,128]{2,1,0:T(8,128)(2,1)S(1)}, u32[]{:S(2)}, u32[]{:S(2)}) collective-permute-start(bf16[1,128,128]{2,1,0:T(8,128)(2,1)S(1)} %get-tuple-element.54), channel_id=1, source_target_pairs={{2,0},{4,2},{6,4},{8,6},{10,8},{12,10},{14,12},{16,14},{18,16},{20... | collective-permute-start | bytes 98312 | tf_op jit(solution)/shard_map/ppermute | solution.py:18
  75.8 8.2 %copy-start.11 = (f32[128]{0:T(128)S(1)}, f32[128]{0:T(128)}, u32[]{:S(2)}) copy-start(f32[128]{0:T(128)} %get-tuple-element.74) | copy-start | bytes 1540
  75.8 8.2 %copy-start.12 = (f32[128]{0:T(128)S(1)}, f32[128]{0:T(128)}, u32[]{:S(2)}) copy-start(f32[128]{0:T(128)} %get-tuple-element.75) | copy-start | bytes 1540
  75.8 8.2 %copy-start.13 = (f32[128]{0:T(128)S(1)}, f32[128]{0:T(128)}, u32[]{:S(2)}) copy-start(f32[128]{0:T(128)} %get-tuple-element.76) | copy-start | bytes 1540
  75.8 8.2 %copy-start.14 = (f32[128]{0:T(128)S(1)}, f32[128]{0:T(128)}, u32[]{:S(2)}) copy-start(f32[128]{0:T(128)} %get-tuple-element.77) | copy-start | bytes 1540
  75.8 8.2 %copy-start.15 = (f32[128]{0:T(128)S(1)}, f32[128]{0:T(128)}, u32[]{:S(2)}) copy-start(f32[128]{0:T(128)} %get-tuple-element.78) | copy-start | bytes 1540
  75.8 8.2 %copy-start.16 = (f32[128]{0:T(128)S(1)}, f32[128]{0:T(128)}, u32[]{:S(2)}) copy-start(f32[128]{0:T(128)} %get-tuple-element.79) | copy-start | bytes 1540
  76.0 6.5 %collective-permute-start.4 = (bf16[1,128]{1,0:T(2,128)(2,1)S(1)}, bf16[1,128]{1,0:T(2,128)(2,1)S(1)}, u32[]{:S(2)}, u32[]{:S(2)}) collective-permute-start(bf16[1,128]{1,0:T(2,128)(2,1)S(1)} %get-tuple-element.87), channel_id=1, source_target_pairs={{0,2},{2,4},{4,6},{6,8},{8,10},{10,12},{12,14},{14,16},{16,18},{18... | collective-permute-start | bytes 776 | tf_op jit(solution)/shard_map/ppermute | solution.py:15
  80.8 3.0 %collective-permute-start.5 = (bf16[1,128]{1,0:T(2,128)(2,1)S(1)}, bf16[1,128]{1,0:T(2,128)(2,1)S(1)}, u32[]{:S(2)}, u32[]{:S(2)}) collective-permute-start(bf16[1,128]{1,0:T(2,128)(2,1)S(1)} %get-tuple-element.88), channel_id=1, source_target_pairs={{2,0},{4,2},{6,4},{8,6},{10,8},{12,10},{14,12},{16,14},{18,16},{20... | collective-permute-start | bytes 776 | tf_op jit(solution)/shard_map/ppermute | solution.py:18
  82.4 3.5 %copy-start.7 = (bf16[2,128,128]{1,2,0:T(8,128)(2,1)S(1)}, bf16[2,128,128]{1,2,0:T(8,128)(2,1)}, u32[]{:S(2)}) copy-start(bf16[2,128,128]{1,2,0:T(8,128)(2,1)} %copy-done.6) | copy-start | bytes 196612
  86.6 0.8 copy-start.5
  88.0 0.8 copy-start.3
  (3 other events, 2.0 us)
Sparse Core Ops, SparseCore 0:
  88.9 57.6 reduce-scatter.3
